TPU v7x, 32 devices: a whole 2x2x4 slice. The times are simulated.
32 devices in a mesh: tm: 8 (over z, x), user: 4 (over y, core).
Axes of the slice: x: 2, y: 2, z: 4, core: 2. Of those that a mesh axis runs over, the one named last changes fastest.
Arguments:
- user_factor: bfloat16 [8192, 128], P('user'), may hold values from -2.390625 to 2.390625
- user_tangent: bfloat16 [8192, 128], P('user'), may hold values from -2.390625 to 2.390625
- item_factor: bfloat16 [512, 128], P('tm'), may hold values from -2.390625 to 2.390625
- item_tangent: bfloat16 [512, 128], P('tm'), may hold values from -2.390625 to 2.390625
- time_factor: bfloat16 [128, 128], P('tm'), may hold values from -2.390625 to 2.390625
- time_tangent: bfloat16 [128, 128], P('tm'), may hold values from -2.390625 to 2.390625
- send_list: int32 [8, 4, 4, 4], P('tm', 'user'), may hold values from 0 to 15
- tile_slot: int32 [8, 4, 16], P('tm', 'user'), may hold values from 0 to 15, as said below
- tile_item: int32 [8, 4, 16], P('tm', 'user'), may hold values from 0 to 1
- tile_count: int32 [8, 4], P('tm', 'user'), may hold values from 8 to 16, as said below
Outputs:
- user_hvp: float32 [8192, 128], P('user')
- item_hvp: float32 [512, 128], P('tm')
- time_hvp: float32 [128, 128], P('tm')
Inputs may be any that keep to these rules, and one draw needn't show every extreme that they name: `tile_slot`: for each (a, j) the first min(16, 16) entries are distinct. `tile_count`: some pair (a, j) has exactly 16 tiles in every draw.
All inputs are finite; a program needn't handle non-finite values.
Results may differ from a plain program's by a relative error of at most 0.0013.
Values may be sent and summed in bfloat16 or wider, within the bound.
No kernel may reach another device: no remote copies, remote signals or barrier semaphores. Data moves between devices by JAX's collectives and lax.ppermute only.
A program may use at most 64 MiB of HBM per device.

v0:
```python
import jax
import jax.numpy as jnp
from jax import lax
from jax.sharding import PartitionSpec as P

R = 128
UB = 128
IT = 256
NT_CAP = 16
OBS_WEIGHT = 0.03125
LAMBDA_USER = 0.5
LAMBDA_ITEM = 0.5
LAMBDA_TIME = 1.0


def with_halo(cells, sides, width):
    for axis, dim in sides:
        count = lax.axis_size(axis)
        ends = count - 1
        head = lax.slice_in_dim(cells, 0, width, axis=dim)
        tail = lax.slice_in_dim(cells, cells.shape[dim] - width, cells.shape[dim], axis=dim)
        cells = jnp.concatenate(
            [
                lax.ppermute(tail, axis, [(i, (i + 1) % count) for i in range(ends)]),
                cells,
                lax.ppermute(head, axis, [((i + 1) % count, i) for i in range(ends)]),
            ],
            axis=dim,
        )
    return cells


def tile_terms(user_block, user_delta, item_block, item_delta, time_rows, time_delta):
    factor_u = user_block.astype(jnp.float32)
    delta_u = user_delta.astype(jnp.float32)
    scaled = (factor_u[None] * time_rows[:, None, :]).astype(jnp.bfloat16)
    mixed = (
        delta_u[None] * time_rows[:, None, :] + factor_u[None] * time_delta[:, None, :]
    ).astype(jnp.bfloat16)
    left_side = jnp.concatenate([mixed, scaled], axis=-1)
    right_side = jnp.concatenate([item_block, item_delta], axis=-1)
    change = jnp.einsum(
        "tuk,ik->tui", left_side, right_side, preferred_element_type=jnp.float32
    ).astype(jnp.bfloat16)
    projected = jnp.einsum("tui,ir->tur", change, item_block, preferred_element_type=jnp.float32)
    user_term = jnp.sum(projected * time_rows[:, None, :], axis=0)
    time_term = jnp.sum(projected * factor_u[None], axis=1)
    item_term = jnp.einsum("tui,tur->ir", change, scaled, preferred_element_type=jnp.float32)
    return (user_term, item_term, time_term)


def add_tile(
    number,
    carry,
    weight,
    slot_blocks,
    slot_deltas,
    all_items,
    all_deltas,
    time_rows,
    time_delta,
    slots,
    item_ids,
):
    slot_acc, item_acc, time_acc = carry
    where = slots[number]
    which = item_ids[number] * IT
    user_block = lax.dynamic_index_in_dim(slot_blocks, where, 0, keepdims=False)
    user_delta = lax.dynamic_index_in_dim(slot_deltas, where, 0, keepdims=False)
    item_block = lax.dynamic_slice_in_dim(all_items, which, IT, 0)
    item_delta = lax.dynamic_slice_in_dim(all_deltas, which, IT, 0)
    user_term, item_term, time_term = tile_terms(
        user_block, user_delta, item_block, item_delta, time_rows, time_delta
    )
    slot_acc = slot_acc.at[where].add(weight * user_term)
    current = lax.dynamic_slice_in_dim(item_acc, which, IT, 0)
    item_acc = lax.dynamic_update_slice_in_dim(item_acc, current + weight * item_term, which, 0)
    time_acc = time_acc + weight * time_term
    return (slot_acc, item_acc, time_acc)


def body(
    user_factor,
    user_tangent,
    item_factor,
    item_tangent,
    time_factor,
    time_tangent,
    send_list,
    tile_slot,
    tile_item,
    tile_count,
):
    all_items, all_deltas = (
        lax.all_gather(item_factor, "tm", axis=0, tiled=True),
        lax.all_gather(item_tangent, "tm", axis=0, tiled=True),
    )
    block_rows = user_factor.shape[0] // UB
    peers = lax.axis_size("user")
    home_blocks = user_factor.reshape(block_rows, UB, R)
    home_deltas = user_tangent.reshape(block_rows, UB, R)
    chosen = send_list[0, 0]
    got_blocks, got_deltas = (
        lax.all_to_all(home_blocks[chosen], "user", split_axis=0, concat_axis=0, tiled=True),
        lax.all_to_all(home_deltas[chosen], "user", split_axis=0, concat_axis=0, tiled=True),
    )
    slot_blocks = got_blocks.reshape(-1, UB, R)
    slot_deltas = got_deltas.reshape(-1, UB, R)
    time_rows = time_factor.astype(jnp.float32)
    time_delta = time_tangent.astype(jnp.float32)
    slots = tile_slot[0, 0]
    item_ids = tile_item[0, 0]
    count = tile_count[0, 0]
    start = (
        jnp.zeros(slot_blocks.shape, jnp.float32),
        jnp.zeros(all_items.shape, jnp.float32),
        jnp.zeros(time_rows.shape, jnp.float32),
    )

    def padded_tile(number, carry):
        weight = OBS_WEIGHT * (number < count).astype(jnp.float32)
        return add_tile(
            number,
            carry,
            weight,
            slot_blocks,
            slot_deltas,
            all_items,
            all_deltas,
            time_rows,
            time_delta,
            slots,
            item_ids,
        )

    slot_acc, item_acc, time_acc = lax.fori_loop(0, NT_CAP, padded_tile, start)
    returned = lax.all_to_all(
        slot_acc.reshape(peers, -1, UB, R), "user", split_axis=0, concat_axis=0, tiled=True
    )
    flat_ids = send_list[0, 0].reshape(-1)
    table = (jnp.arange(block_rows, dtype=jnp.int32)[:, None] == flat_ids[None, :]).astype(
        jnp.float32
    )
    home_grads = jnp.dot(
        table,
        returned.reshape(flat_ids.shape[0], -1),
        precision=lax.Precision.HIGHEST,
        preferred_element_type=jnp.float32,
    ).reshape(-1, R)
    user_hvp = lax.psum(home_grads, "tm") + LAMBDA_USER * user_tangent.astype(jnp.float32)
    piece = lax.psum_scatter(item_acc, "tm", scatter_dimension=0, tiled=True)
    piece, time_acc = lax.psum((piece, time_acc), "user")
    item_hvp = piece + LAMBDA_ITEM * item_tangent.astype(jnp.float32)
    steps_here = time_tangent.shape[0]
    extended = with_halo(time_tangent, (("tm", 0),), 2).astype(jnp.float32)
    second = extended[:-2] - 2.0 * extended[1:-1] + extended[2:]
    position = lax.axis_index("tm") * steps_here - 1 + jnp.arange(steps_here + 2, dtype=jnp.int32)
    total_steps = steps_here * lax.axis_size("tm")
    interior = (position >= 1) & (position <= total_steps - 2)
    second = jnp.where(interior[:, None], second, 0.0)
    penalty = second[:-2] - 2.0 * second[1:-1] + second[2:]
    time_hvp = time_acc + LAMBDA_TIME * penalty
    return (user_hvp, item_hvp, time_hvp)


def solution(mesh):
    return jax.shard_map(
        body,
        mesh=mesh,
        in_specs=(
            P("user", None),
            P("user", None),
            P("tm", None),
            P("tm", None),
            P("tm", None),
            P("tm", None),
            P("tm", "user", None, None),
            P("tm", "user", None),
            P("tm", "user", None),
            P("tm", "user"),
        ),
        out_specs=(P("user", None), P("tm", None), P("tm", None)),
        check_vma=False,
    )
```

profile of v0, /device:TPU:0, one launch (start us, length us, event | category | flops | bytes accessed | tf_op | source)
XLA Modules:
  0.0 426.5 jit_solution(17418752064839015805)
XLA Ops:
  8.0 2.4 gather_fusion
  10.5 4.3 all-to-all-start
  16.2 7.4 %all-to-all-done = bf16[4,4,128,128]{3,2,1,0:T(8,128)(2,1)S(1)} async-done(((bf16[4,4,128,128]{3,2,1,0:T(8,128)(2,1)}), bf16[4,4,128,128]{3,2,1,0:T(8,128)(2,1)S(1)}, u32[]{:S(2)}, u32[]{:S(2)}) %all-to-all-start) | async-done | bytes 524320 | tf_op jit(solution)/shard_map/all_to_all | solution.py:105
  23.5 3.5 all-to-all-start.1
  27.1 31.6 %all_gather.6 = bf16[512,128]{1,0:T(8,128)(2,1)S(1)} all-gather(bf16[64,128]{1,0:T(8,128)(2,1)S(1)} %copy-done.5), channel_id=1, replica_groups=mesh['tm'=8,'user'=4] {'tm'}, dimensions={0}, use_global_device_ids=true | all-gather | bytes 147456 | tf_op jit(solution)/shard_map/all_gather | solution.py:95
  58.7 30.5 %all_gather.7 = bf16[512,128]{1,0:T(8,128)(2,1)S(1)} all-gather(bf16[64,128]{1,0:T(8,128)(2,1)S(1)} %copy-done.3), channel_id=1, replica_groups=mesh['tm'=8,'user'=4] {'tm'}, dimensions={0}, use_global_device_ids=true | all-gather | bytes 147456 | tf_op jit(solution)/shard_map/all_gather | solution.py:96
  90.4 173.7 %while.19 = (s32[]{:T(128)}, f32[16,128,128]{2,1,0:T(8,128)}, f32[512,128]{1,0:T(8,128)S(1)}, f32[16,128]{1,0:T(8,128)S(1)}, s32[16]{0:T(128)S(1)}, /*index=5*/s...) while((s32[]{:T(128)}, f32[16,128,128]{2,1,0:T(8,128)}, ...), condition=%wide.region_4.5_spmd.clone, body=%wide.region_0.4_spmd.clone.sunk | while | flops 543035392 | bytes 10945942 | solution.py:136
  97.4 2.1 fusion.31
  99.5 1.7 fusion.32
  108.2 2.1 fusion.31
  119.1 2.1 fusion.31
  129.9 2.1 fusion.31
  140.8 2.1 fusion.31
  151.7 2.1 fusion.31
  162.5 2.1 fusion.31
  173.4 2.1 fusion.31
  184.2 2.1 fusion.31
  195.1 2.1 fusion.31
  205.9 2.1 fusion.31
  216.8 2.1 fusion.31
  227.6 2.1 fusion.31
  238.5 2.1 fusion.31
  249.3 2.1 fusion.31
  260.2 2.1 fusion.31
  264.8 3.5 all-to-all-start.2
  269.2 13.5 %all-to-all-done.2 = f32[4,4,128,128]{3,2,1,0:T(8,128)S(1)} async-done(((f32[4,4,128,128]{3,2,1,0:T(8,128)}), f32[4,4,128,128]{3,2,1,0:T(8,128)S(1)}, u32[]{:S(2)}, u32[]{:S(2)}) %all-to-all-start.2) | async-done | bytes 1048608 | tf_op jit(solution)/shard_map/all_to_all | solution.py:137
  285.1 3.4 collective-permute-start
  289.9 4.1 collective-permute-done.1
  294.1 41.8 %reduce-scatter.2.cloned.1.call-done = f32[64,128]{1,0:T(8,128)} async-done(((f32[512,128]{1,0:T(8,128)}), f32[64,128]{1,0:T(8,128)}) %reduce-scatter.2.cloned.1.call-update) | async-done | bytes 32784 | tf_op jit(solution)/shard_map/reduce_scatter | solution.py:151
  335.9 11.0 %all-reduce = (f32[64,128]{1,0:T(8,128)S(1)}, f32[16,128]{1,0:T(8,128)S(1)}) all-reduce(f32[64,128]{1,0:T(8,128)} %reduce-scatter.2.cloned.1.call-done, f32[16,128]{1,0:T(8,128)S(1)} %get-tuple-element.243), channel_id=1, replica_groups=mesh['tm'=8,'user'=4] {'user'}, use_global_device_ids=true, to_apply=%region_7.8 | all-reduce | flops 10240 | bytes 81920 | tf_op jit(solution)/shard_map/psum | solution.py:152
  348.2 69.2 %all-reduce.3.cloned.1.call-done = f32[2048,128]{1,0:T(8,128)} async-done(((f32[2048,128]{1,0:T(8,128)}), f32[2048,128]{1,0:T(8,128)}) %all-reduce.3.cloned.1.call-update) | async-done | bytes 1048592 | tf_op jit(solution)/shard_map/psum | solution.py:150
  417.4 2.3 multiply_add_fusion
  (238 shorter events, 95.2 us)
Async XLA Ops:
  7.2 7.6 %copy-start = (bf16[2048,128]{1,0:T(8,128)(2,1)S(1)}, bf16[2048,128]{1,0:T(8,128)(2,1)}, u32[]{:S(2)}) copy-start(bf16[2048,128]{1,0:T(8,128)(2,1)} %param.14) | copy-start | bytes 1572868
  10.5 13.1 %all-to-all-start = ((bf16[4,4,128,128]{3,2,1,0:T(8,128)(2,1)}), bf16[4,4,128,128]{3,2,1,0:T(8,128)(2,1)S(1)}, u32[]{:S(2)}, u32[]{:S(2)}) async-start(bf16[4,4,128,128]{3,2,1,0:T(8,128)(2,1)} %bitcast.4), calls=%async_computation | async-start | bytes 1048576 | tf_op jit(solution)/shard_map/all_to_all | solution.py:105
  14.7 12.3 %copy-start.8 = (bf16[16,128]{1,0:T(8,128)(2,1)S(1)}, bf16[16,128]{1,0:T(8,128)(2,1)}, u32[]{:S(2)}) copy-start(bf16[16,128]{1,0:T(8,128)(2,1)} %param.18) | copy-start | bytes 12292
  14.7 12.4 %copy-start.4 = (bf16[16,128]{1,0:T(8,128)(2,1)S(1)}, bf16[16,128]{1,0:T(8,128)(2,1)}, u32[]{:S(2)}) copy-start(bf16[16,128]{1,0:T(8,128)(2,1)} %param.19) | copy-start | bytes 12292
  14.7 12.4 %copy-start.5 = (bf16[64,128]{1,0:T(8,128)(2,1)S(1)}, bf16[64,128]{1,0:T(8,128)(2,1)}, u32[]{:S(2)}) copy-start(bf16[64,128]{1,0:T(8,128)(2,1)} %param.16) | copy-start | bytes 49156
  14.8 44.0 %copy-start.3 = (bf16[64,128]{1,0:T(8,128)(2,1)S(1)}, bf16[64,128]{1,0:T(8,128)(2,1)}, u32[]{:S(2)}) copy-start(bf16[64,128]{1,0:T(8,128)(2,1)} %param.17) | copy-start | bytes 49156
  23.5 65.7 %all-to-all-start.1 = ((bf16[4,4,128,128]{3,2,1,0:T(8,128)(2,1)}), bf16[4,4,128,128]{3,2,1,0:T(8,128)(2,1)S(1)}, u32[]{:S(2)}, u32[]{:S(2)}) async-start(bf16[4,4,128,128]{3,2,1,0:T(8,128)(2,1)} %bitcast.7), calls=%async_computation.1 | async-start | bytes 1048576 | tf_op jit(solution)/shard_map/all_to_all | solution.py:104
  27.0 63.3 %copy-start.6 = (s32[3]{0:T(128)S(1)}, s32[3]{0:T(128)}, u32[]{:S(2)}) copy-start(s32[3]{0:T(128)} %constant.113.clone.2) | copy-start | bytes 40
  27.0 63.3 %copy-start.9 = (s32[1,1,16]{2,1,0:T(1,128)S(1)}, s32[1,1,16]{2,1,0:T(1,128)}, u32[]{:S(2)}) copy-start(s32[1,1,16]{2,1,0:T(1,128)} %param.21) | copy-start | bytes 196
  27.0 63.3 %copy-start.10 = (s32[1,1,16]{2,1,0:T(1,128)S(1)}, s32[1,1,16]{2,1,0:T(1,128)}, u32[]{:S(2)}) copy-start(s32[1,1,16]{2,1,0:T(1,128)} %param.22) | copy-start | bytes 196
  95.0 1.0 copy-start.11
  105.9 1.0 copy-start.11
  116.7 1.0 copy-start.11
  127.6 1.0 copy-start.11
  138.4 1.0 copy-start.11
  149.3 1.0 copy-start.11
  160.1 1.0 copy-start.11
  171.0 1.0 copy-start.11
  181.8 1.0 copy-start.11
  192.7 1.0 copy-start.11
  203.6 1.0 copy-start.11
  214.4 1.0 copy-start.11
  225.3 1.0 copy-start.11
  236.1 1.0 copy-start.11
  257.8 1.0 copy-start.11
  264.1 5.0 %copy-start.7 = (s32[1,1,4,4]{3,2,1,0:T(4,128)S(1)}, s32[1,1,4,4]{3,2,1,0:T(4,128)}, u32[]{:S(2)}) copy-start(s32[1,1,4,4]{3,2,1,0:T(4,128)} %param.20) | copy-start | bytes 196
  264.8 17.9 %all-to-all-start.2 = ((f32[4,4,128,128]{3,2,1,0:T(8,128)}), f32[4,4,128,128]{3,2,1,0:T(8,128)S(1)}, u32[]{:S(2)}, u32[]{:S(2)}) async-start(f32[4,4,128,128]{3,2,1,0:T(8,128)} %bitcast.10), calls=%async_computation.2 | async-start | bytes 2097152 | tf_op jit(solution)/shard_map/all_to_all | solution.py:137
  268.3 67.6 %reduce-scatter.2.cloned.1.call-start = ((), (), s32[]{:S(2)}) async-start(), calls=%async_computation.5 | async-start | bytes 294912 | tf_op jit(solution)/shard_map/reduce_scatter | solution.py:151
  269.0 148.3 %all-reduce.3.cloned.1.call-start = ((), (), s32[]{:S(2)}) async-start(), calls=%async_computation.4 | async-start | bytes 2097152 | tf_op jit(solution)/shard_map/psum | solution.py:150
  285.0 132.3 %copy-start.1 = (bf16[2048,128]{1,0:T(8,128)(2,1)S(1)}, bf16[2048,128]{1,0:T(8,128)(2,1)}, u32[]{:S(2)}) copy-start(bf16[2048,128]{1,0:T(8,128)(2,1)} %param.15) | copy-start | bytes 1572868
  285.1 4.8 %collective-permute-start = (bf16[2,128]{1,0:T(2,128)(2,1)S(1)}, bf16[2,128]{1,0:T(2,128)(2,1)S(1)}, u32[]{:S(2)}, u32[]{:S(2)}) collective-permute-start(bf16[2,128]{1,0:T(2,128)(2,1)S(1)} %get-tuple-element.322), channel_id=1, source_target_pairs={{0,4},{4,8},{8,12},{12,16},{16,20},{20,24},{24,28},{1,5},{5,9},{9,... | collective-permute-start | bytes 1544 | tf_op jit(solution)/shard_map/ppermute | solution.py:24
  288.5 5.5 %collective-permute-start.1 = (bf16[2,128]{1,0:T(2,128)(2,1)S(1)}, bf16[2,128]{1,0:T(2,128)(2,1)S(1)}, u32[]{:S(2)}, u32[]{:S(2)}) collective-permute-start(bf16[2,128]{1,0:T(2,128)(2,1)S(1)} %get-tuple-element.323), channel_id=1, source_target_pairs={{4,0},{8,4},{12,8},{16,12},{20,16},{24,20},{28,24},{5,1},{9,5},{13... | collective-permute-start | bytes 1544 | tf_op jit(solution)/shard_map/ppermute | solution.py:26
  (2 other events, 1.7 us)
Sparse Core Ops, SparseCore 0:
  272.4 63.4 reduce-scatter.1
  340.0 77.3 all-reduce.2
where the time goes:
time: 429 us; the launch traced here: 427 us
  waiting for transfers between devices  137 us (32%)
  blocking collectives  73.1 us (17%)
  other arithmetic  55 us (13%)
  loops' own time  52.9 us (12%)
  matrix products  43.1 us (10%)
  local copies, waits for them, and re-layouts  35.2 us (8%)
  starting transfers between devices  16.1 us (4%)
  between operations  14.3 us (3%)
    psum x1, waiting for transfers between devices, body(): lax.psum(home_grads, 'tm') + LAMBDA_USER * user_tangent.astype(jnp.float32)  69.2 us
    another operation x1, loops' own time, body(): slot_acc, item_acc, time_acc = lax.fori_loop(0, NT_CAP, padded_tile, start)  52.9 us
    reduce_scatter x1, waiting for transfers between devices, body(): piece = lax.psum_scatter(item_acc, 'tm', scatter_dimension=0, tiled=True)  41.8 us
    scatter-add x16, other arithmetic, add_tile(): slot_acc = slot_acc.at[where].add(weight * user_term)  33.7 us
    all_gather x1, blocking collectives, body(): lax.all_gather(item_factor, 'tm', axis=0, tiled=True)  31.6 us
    all_gather x1, blocking collectives, body(): lax.all_gather(item_tangent, 'tm', axis=0, tiled=True)  30.5 us
    dot_general x16, matrix products, tile_terms(): jnp.einsum('tui,tur->ir', change, scaled, preferred_element_type=jnp.floa...  27.3 us
    all_to_all x1, waiting for transfers between devices, body(): lax.all_to_all(slot_acc.reshape(peers, -1, UB, R), 'user', split_axis=0,...  13.5 us
  transfers between devices with their start and end apart: 7, of which 5 were waited for; matrix products, arithmetic and copies ran while one was open for 1% of the time, Pallas kernels for 0%

commit v1 on v0

--- a/solution.py
+++ b/solution.py
@@ -147,7 +147,9 @@
         precision=lax.Precision.HIGHEST,
         preferred_element_type=jnp.float32,
     ).reshape(-1, R)
-    user_hvp = lax.psum(home_grads, "tm") + LAMBDA_USER * user_tangent.astype(jnp.float32)
+    user_hvp = jnp.sum(
+        lax.all_gather(home_grads, "tm"), axis=0
+    ) + LAMBDA_USER * user_tangent.astype(jnp.float32)
     piece = lax.psum_scatter(item_acc, "tm", scatter_dimension=0, tiled=True)
     piece, time_acc = lax.psum((piece, time_acc), "user")
     item_hvp = piece + LAMBDA_ITEM * item_tangent.astype(jnp.float32)

time: 429 us -> 446 us (1.040)
  waiting for transfers between devices: 137 us -> 182 us
  matrix products: 43.1 us -> 23.5 us
  local copies, waits for them, and re-layouts: 35.2 us -> 24.9 us
    all_gather x0 -> x1, waiting for transfers between devices: none -> 114 us  [body(): lax.all_gather(home_grads, 'tm')]
    psum x1 -> x0, waiting for transfers between devices: 69.2 us -> none  [body(): lax.psum(home_grads, 'tm') + LAMBDA_USER * user_tangent.astype(jnp.float32)]
    dot_general x16, matrix products: 27.3 us -> 7.74 us  [tile_terms(): jnp.einsum('tui,tur->ir', change, scaled, preferred_element_type=jnp.floa...]
    while x32 -> x0, local copies, waits for them, and re-layouts: 8.19 us -> none
    all_to_all x1, waiting for transfers between devices: 0.01 us -> 7.39 us  [body(): lax.all_to_all(home_blocks[chosen], 'user', split_axis=0, concat_axis=0,...]
    all_to_all x1, waiting for transfers between devices: 7.37 us -> 0.01 us  [body(): lax.all_to_all(home_deltas[chosen], 'user', split_axis=0, concat_axis=0,...]
where the time goes in v1:
time: 446 us; the launch traced here: 444 us
  waiting for transfers between devices  182 us (41%)
  blocking collectives  73.1 us (16%)
  other arithmetic  57.8 us (13%)
  loops' own time  52.5 us (12%)
  local copies, waits for them, and re-layouts  24.9 us (6%)
  matrix products  23.5 us (5%)
  starting transfers between devices  16.1 us (4%)
  between operations  14.2 us (3%)
    all_gather x1, waiting for transfers between devices, body(): lax.all_gather(home_grads, 'tm')  114 us
    another operation x1, loops' own time, body(): slot_acc, item_acc, time_acc = lax.fori_loop(0, NT_CAP, padded_tile, start)  52.5 us
    reduce_scatter x1, waiting for transfers between devices, body(): piece = lax.psum_scatter(item_acc, 'tm', scatter_dimension=0, tiled=True)  41.9 us
    scatter-add x16, other arithmetic, add_tile(): slot_acc = slot_acc.at[where].add(weight * user_term)  33.8 us
    all_gather x1, blocking collectives, body(): lax.all_gather(item_factor, 'tm', axis=0, tiled=True)  31.6 us
    all_gather x1, blocking collectives, body(): lax.all_gather(item_tangent, 'tm', axis=0, tiled=True)  30.5 us
    all_to_all x1, waiting for transfers between devices, body(): lax.all_to_all(slot_acc.reshape(peers, -1, UB, R), 'user', split_axis=0,...  13.5 us
    another operation x16, other arithmetic  11.9 us
  transfers between devices with their start and end apart: 7, of which 5 were waited for; matrix products, arithmetic and copies ran while one was open for 1% of the time, Pallas kernels for 0%

profile of v1, /device:TPU:0, one launch (start us, length us, event | category | flops | bytes accessed | tf_op | source)
XLA Modules:
  0.0 443.8 jit_solution(821496694631253448)
XLA Ops:
  8.2 1.4 gather_fusion.1
  9.6 4.3 all-to-all-start.1
  13.9 1.4 gather_fusion
  15.3 7.4 %all-to-all-done.1 = bf16[4,4,128,128]{3,2,1,0:T(8,128)(2,1)S(1)} async-done(((bf16[4,4,128,128]{3,2,1,0:T(8,128)(2,1)}), bf16[4,4,128,128]{3,2,1,0:T(8,128)(2,1)S(1)}, u32[]{:S(2)}, u32[]{:S(2)}) %all-to-all-start.1) | async-done | bytes 524320 | tf_op jit(solution)/shard_map/all_to_all | solution.py:104
  22.7 3.5 all-to-all-start
  26.3 31.6 %all_gather.9 = bf16[512,128]{1,0:T(8,128)(2,1)S(1)} all-gather(bf16[64,128]{1,0:T(8,128)(2,1)S(1)} %copy-done.5), channel_id=1, replica_groups=mesh['tm'=8,'user'=4] {'tm'}, dimensions={0}, use_global_device_ids=true | all-gather | bytes 147456 | tf_op jit(solution)/shard_map/all_gather | solution.py:95
  57.9 30.5 %all_gather.10 = bf16[512,128]{1,0:T(8,128)(2,1)S(1)} all-gather(bf16[64,128]{1,0:T(8,128)(2,1)S(1)} %copy-done.3), channel_id=1, replica_groups=mesh['tm'=8,'user'=4] {'tm'}, dimensions={0}, use_global_device_ids=true | all-gather | bytes 147456 | tf_op jit(solution)/shard_map/all_gather | solution.py:96
  89.5 145.0 %while.19 = (s32[]{:T(128)}, f32[16,128,128]{2,1,0:T(8,128)}, f32[512,128]{1,0:T(8,128)S(1)}, f32[16,128]{1,0:T(8,128)S(1)}, s32[16]{0:T(128)S(1)}, /*index=5*/s...) while((s32[]{:T(128)}, f32[16,128,128]{2,1,0:T(8,128)}, ...), condition=%wide.region_4.5_spmd.clone, body=%wide.region_0.4_spmd.clone.sunk | while | flops 543035392 | bytes 6751618 | solution.py:136
  96.5 2.1 fusion.31
  105.5 2.1 fusion.31
  114.6 2.1 fusion.31
  123.6 2.1 fusion.31
  132.7 2.1 fusion.31
  141.8 2.1 fusion.31
  150.8 2.1 fusion.31
  159.9 2.1 fusion.31
  169.0 2.1 fusion.31
  178.0 2.1 fusion.31
  187.1 2.1 fusion.31
  196.2 2.1 fusion.31
  205.2 2.1 fusion.31
  214.3 2.1 fusion.31
  223.4 2.1 fusion.31
  232.4 2.1 fusion.31
  234.5 3.6 all-to-all-start.2
  239.1 13.5 %all-to-all-done.2 = f32[4,4,128,128]{3,2,1,0:T(8,128)S(1)} async-done(((f32[4,4,128,128]{3,2,1,0:T(8,128)}), f32[4,4,128,128]{3,2,1,0:T(8,128)S(1)}, u32[]{:S(2)}, u32[]{:S(2)}) %all-to-all-start.2) | async-done | bytes 1048608 | tf_op jit(solution)/shard_map/all_to_all | solution.py:137
  255.0 3.3 collective-permute-start
  259.6 4.1 collective-permute-done.1
  263.9 41.9 %reduce-scatter.2.cloned.1.call-done = f32[64,128]{1,0:T(8,128)} async-done(((f32[512,128]{1,0:T(8,128)}), f32[64,128]{1,0:T(8,128)}) %reduce-scatter.2.cloned.1.call-update) | async-done | bytes 32784 | tf_op jit(solution)/shard_map/reduce_scatter | solution.py:153
  305.7 11.0 %all-reduce = (f32[64,128]{1,0:T(8,128)S(1)}, f32[16,128]{1,0:T(8,128)S(1)}) all-reduce(f32[64,128]{1,0:T(8,128)} %reduce-scatter.2.cloned.1.call-done, f32[16,128]{1,0:T(8,128)S(1)} %get-tuple-element.243), channel_id=1, replica_groups=mesh['tm'=8,'user'=4] {'user'}, use_global_device_ids=true, to_apply=%region_7.8 | all-reduce | flops 10240 | bytes 81920 | tf_op jit(solution)/shard_map/psum | solution.py:154
  318.0 114.0 %all-gather.2.cloned.1.call-done = f32[8,2048,128]{2,1,0:T(8,128)} async-done(((f32[1,2048,128]{2,1,0:T(8,128)}), f32[8,2048,128]{2,1,0:T(8,128)}) %all-gather.2.cloned.1.call-update) | async-done | bytes 8388624 | tf_op jit(solution)/shard_map/all_gather | solution.py:151
  432.0 3.9 reduce_sum.35
  (207 shorter events, 67.8 us)
Async XLA Ops:
  7.2 1.1 copy-start
  7.2 6.7 %copy-start.1 = (bf16[2048,128]{1,0:T(8,128)(2,1)S(1)}, bf16[2048,128]{1,0:T(8,128)(2,1)}, u32[]{:S(2)}) copy-start(bf16[2048,128]{1,0:T(8,128)(2,1)} %param.15) | copy-start | bytes 1572868
  8.2 18.0 %copy-start.8 = (bf16[16,128]{1,0:T(8,128)(2,1)S(1)}, bf16[16,128]{1,0:T(8,128)(2,1)}, u32[]{:S(2)}) copy-start(bf16[16,128]{1,0:T(8,128)(2,1)} %param.18) | copy-start | bytes 12292
  8.2 18.0 %copy-start.4 = (bf16[16,128]{1,0:T(8,128)(2,1)S(1)}, bf16[16,128]{1,0:T(8,128)(2,1)}, u32[]{:S(2)}) copy-start(bf16[16,128]{1,0:T(8,128)(2,1)} %param.19) | copy-start | bytes 12292
  8.2 18.0 %copy-start.5 = (bf16[64,128]{1,0:T(8,128)(2,1)S(1)}, bf16[64,128]{1,0:T(8,128)(2,1)}, u32[]{:S(2)}) copy-start(bf16[64,128]{1,0:T(8,128)(2,1)} %param.16) | copy-start | bytes 49156
  8.2 49.6 %copy-start.3 = (bf16[64,128]{1,0:T(8,128)(2,1)S(1)}, bf16[64,128]{1,0:T(8,128)(2,1)}, u32[]{:S(2)}) copy-start(bf16[64,128]{1,0:T(8,128)(2,1)} %param.17) | copy-start | bytes 49156
  9.6 13.1 %all-to-all-start.1 = ((bf16[4,4,128,128]{3,2,1,0:T(8,128)(2,1)}), bf16[4,4,128,128]{3,2,1,0:T(8,128)(2,1)S(1)}, u32[]{:S(2)}, u32[]{:S(2)}) async-start(bf16[4,4,128,128]{3,2,1,0:T(8,128)(2,1)} %bitcast.7), calls=%async_computation.1 | async-start | bytes 1048576 | tf_op jit(solution)/shard_map/all_to_all | solution.py:104
  13.9 75.6 %copy-start.6 = (s32[3]{0:T(128)S(1)}, s32[3]{0:T(128)}, u32[]{:S(2)}) copy-start(s32[3]{0:T(128)} %constant.113.clone.2) | copy-start | bytes 40
  13.9 75.6 %copy-start.9 = (s32[1,1,16]{2,1,0:T(1,128)S(1)}, s32[1,1,16]{2,1,0:T(1,128)}, u32[]{:S(2)}) copy-start(s32[1,1,16]{2,1,0:T(1,128)} %param.21) | copy-start | bytes 196
  13.9 75.6 %copy-start.10 = (s32[1,1,16]{2,1,0:T(1,128)S(1)}, s32[1,1,16]{2,1,0:T(1,128)}, u32[]{:S(2)}) copy-start(s32[1,1,16]{2,1,0:T(1,128)} %param.22) | copy-start | bytes 196
  22.7 65.7 %all-to-all-start = ((bf16[4,4,128,128]{3,2,1,0:T(8,128)(2,1)}), bf16[4,4,128,128]{3,2,1,0:T(8,128)(2,1)S(1)}, u32[]{:S(2)}, u32[]{:S(2)}) async-start(bf16[4,4,128,128]{3,2,1,0:T(8,128)(2,1)} %bitcast.4), calls=%async_computation | async-start | bytes 1048576 | tf_op jit(solution)/shard_map/all_to_all | solution.py:105
  234.5 3.7 copy-start.2
  234.5 4.4 %copy-start.7 = (s32[1,1,4,4]{3,2,1,0:T(4,128)S(1)}, s32[1,1,4,4]{3,2,1,0:T(4,128)}, u32[]{:S(2)}) copy-start(s32[1,1,4,4]{3,2,1,0:T(4,128)} %param.20) | copy-start | bytes 196
  234.5 18.1 %all-to-all-start.2 = ((f32[4,4,128,128]{3,2,1,0:T(8,128)}), f32[4,4,128,128]{3,2,1,0:T(8,128)S(1)}, u32[]{:S(2)}, u32[]{:S(2)}) async-start(f32[4,4,128,128]{3,2,1,0:T(8,128)} %bitcast.10), calls=%async_computation.2 | async-start | bytes 2097152 | tf_op jit(solution)/shard_map/all_to_all | solution.py:137
  238.2 67.5 %reduce-scatter.2.cloned.1.call-start = ((), (), s32[]{:S(2)}) async-start(), calls=%async_computation.5 | async-start | bytes 294912 | tf_op jit(solution)/shard_map/reduce_scatter | solution.py:153
  238.9 193.0 %all-gather.2.cloned.1.call-start = ((), (), s32[]{:S(2)}) async-start(), calls=%async_computation.4 | async-start | bytes 9437184 | tf_op jit(solution)/shard_map/all_gather | solution.py:151
  255.0 4.6 %collective-permute-start = (bf16[2,128]{1,0:T(2,128)(2,1)S(1)}, bf16[2,128]{1,0:T(2,128)(2,1)S(1)}, u32[]{:S(2)}, u32[]{:S(2)}) collective-permute-start(bf16[2,128]{1,0:T(2,128)(2,1)S(1)} %get-tuple-element.322), channel_id=1, source_target_pairs={{0,4},{4,8},{8,12},{12,16},{16,20},{20,24},{24,28},{1,5},{5,9},{9,... | collective-permute-start | bytes 1544 | tf_op jit(solution)/shard_map/ppermute | solution.py:24
  258.3 5.5 %collective-permute-start.1 = (bf16[2,128]{1,0:T(2,128)(2,1)S(1)}, bf16[2,128]{1,0:T(2,128)(2,1)S(1)}, u32[]{:S(2)}, u32[]{:S(2)}) collective-permute-start(bf16[2,128]{1,0:T(2,128)(2,1)S(1)} %get-tuple-element.323), channel_id=1, source_target_pairs={{4,0},{8,4},{12,8},{16,12},{20,16},{24,20},{28,24},{5,1},{9,5},{13... | collective-permute-start | bytes 1544 | tf_op jit(solution)/shard_map/ppermute | solution.py:26
Sparse Core Ops, SparseCore 0:
  242.3 63.3 reduce-scatter.1
  308.4 123.5 all-gather.1
